TPU v7x, 32 devices: a whole 2x2x4 slice. The times are simulated.
32 devices in a mesh: src: 4 (over y, core), rcv: 8 (over z, x).
Axes of the slice: x: 2, y: 2, z: 4, core: 2. Of those that a mesh axis runs over, the one named last changes fastest.
Arguments:
- data: bfloat16 [2, 4096, 4096], P(None, ('src', 'rcv')), may hold values from -0.8984375 to 0.8984375
- fill_mask: int32 [4096, 4096], P(('src', 'rcv')), may hold values 0 or 1
- obliquity: float32 [4096], replicated, may hold values from 0.25 to 4
- aperture: int32 [8, 8, 8], P('src'), may hold values from 0 to 7, as said below
- lengths: int32 [8, 8], P('src', 'rcv'), may hold values from 1 to 8, as said below
Outputs:
- predicted: float32 [2, 4096, 4096], P(None, 'src', 'rcv')
Inputs may be any that keep to these rules, and one draw needn't show every extreme that they name: `aperture`: every entry is a tile index; the 8 entries of one output tile are distinct; only the first lengths entries of a list are used. `lengths`: some output tile uses all 8 entries of its list.
All inputs are finite; a program needn't handle non-finite values. No bound on the sum of `fill_mask` on one device may be relied on, other than what follows from the above.
Results may differ from a plain program's by a relative error of at most 0.0028.
Values may be sent and summed in bfloat16 or wider, within the bound.
No kernel may reach another device: no remote copies, remote signals or barrier semaphores. Data moves between devices by JAX's collectives and lax.ppermute only.
A program may use at most 128 MiB of HBM per device.

v0:
```python
import jax
import jax.numpy as jnp
from jax import lax
from jax.sharding import PartitionSpec as P

TILE_SIZE = 512


def complex_product(left_pair, right_pair):
    left_wide = jnp.concatenate([left_pair[0], left_pair[1]], axis=1)
    upper = jnp.concatenate([right_pair[0], right_pair[1]], axis=1)
    lower = jnp.concatenate([-right_pair[1], right_pair[0]], axis=1)
    right_wide = jnp.concatenate([upper, lower], axis=0)
    return jnp.dot(left_wide, right_wide, preferred_element_type=jnp.float32)


def predict_tile(tile_row, my_lists, slot_count, left_piece, column_data):

    def add_slot(slot_index, summed):
        inner_tile = my_lists[tile_row, slot_index]
        left_pair = left_piece(tile_row, slot_index, inner_tile)
        right_pair = lax.dynamic_slice(
            column_data, (0, inner_tile * TILE_SIZE, 0), (2, TILE_SIZE, TILE_SIZE)
        )
        return summed + complex_product(left_pair, right_pair)

    initial = jnp.zeros((TILE_SIZE, 2 * TILE_SIZE), jnp.float32)
    return -lax.fori_loop(0, slot_count, add_slot, initial)


def local(data, fill_mask, obliquity, aperture, lengths):
    local_rows = data.shape[1]
    station_total = data.shape[2]
    src_count = lax.axis_size("src")
    rcv_count = lax.axis_size("rcv")
    devices = src_count * rcv_count
    blocks = data.reshape(2, 1, local_rows, devices, local_rows)
    arrived = lax.all_to_all(blocks, ("src", "rcv"), split_axis=3, concat_axis=1, tiled=True)
    arrived = arrived.reshape(2, devices, local_rows, local_rows)
    transposed = jnp.transpose(arrived, (0, 3, 1, 2)).reshape(2, local_rows, station_total)
    filled = jnp.where(fill_mask[None] == 1, data, transposed)
    tile_block = lax.all_to_all(filled, "rcv", split_axis=2, concat_axis=1, tiled=True)
    span = tile_block.shape[1]
    gains = lax.dynamic_slice_in_dim(obliquity, lax.axis_index("src") * span, span)
    weighted = (tile_block.astype(jnp.float32) * gains[None, :, None]).astype(jnp.bfloat16)
    column_data = lax.all_gather(weighted, "src", axis=1, tiled=True)
    rcv_index = lax.axis_index("rcv")
    my_lists = lax.dynamic_index_in_dim(aperture, rcv_index, 1, keepdims=False)
    tile_rows = span // TILE_SIZE
    row_data = lax.all_gather(tile_block, "rcv", axis=2, tiled=True)

    def left_piece(tile_row, slot_index, inner_tile):
        return lax.dynamic_slice(
            row_data, (0, tile_row * TILE_SIZE, inner_tile * TILE_SIZE), (2, TILE_SIZE, TILE_SIZE)
        )

    results = []
    for tile_row in range(tile_rows):
        results.append(
            predict_tile(tile_row, my_lists, lengths[tile_row, 0], left_piece, column_data)
        )
    stacked = jnp.stack(results).reshape(tile_rows, TILE_SIZE, 2, TILE_SIZE)
    return jnp.transpose(stacked, (2, 0, 1, 3)).reshape(2, tile_rows * TILE_SIZE, TILE_SIZE)


def solution(mesh):
    placed = (
        P(None, ("src", "rcv"), None),
        P(("src", "rcv"), None),
        P(),
        P("src", None, None),
        P("src", "rcv"),
    )
    return jax.shard_map(
        local, mesh=mesh, in_specs=placed, out_specs=P(None, "src", "rcv"), check_vma=False
    )
```

profile of v0, /device:TPU:6, one launch (start us, length us, event | category | flops | bytes accessed | tf_op | source)
XLA Modules:
  0.0 575.6 jit_solution(8887815864550951217)
XLA Ops:
  6.5 3.1 copy.19
  11.1 6.1 %all-to-all-start = ((bf16[2,1,128,32,128]{2,4,0,1,3:T(8,128)(2,1)}), bf16[2,1,128,32,128]{2,4,0,1,3:T(8,128)(2,1)}, u32[]{:S(2)}, u32[]{:S(2)}) async-start(bf16[2,1,128,32,128]{2,4,0,1,3:T(8,128)(2,1)} %copy.17), calls=%async_computation | async-start | bytes 4194304 | tf_op jit(solution)/shard_map/all_to_all | solution.py:38
  17.3 1.9 broadcast_compare_fusion
  20.2 45.0 %all-to-all-done = bf16[2,1,128,32,128]{2,4,0,1,3:T(8,128)(2,1)} async-done(((bf16[2,1,128,32,128]{2,4,0,1,3:T(8,128)(2,1)}), bf16[2,1,128,32,128]{2,4,0,1,3:T(8,128)(2,1)}, u32[]{:S(2)}, u32[]{:S(2)}) %all-to-all-start) | async-done | bytes 2097184 | tf_op jit(solution)/shard_map/all_to_all | solution.py:38
  65.1 4.1 copy.18
  69.2 2.1 broadcast_select_fusion
  71.3 18.1 %copy.20 = bf16[2,128,4096]{1,0,2:T(2,128)(2,1)} copy(bf16[2,128,4096]{1,2,0:T(8,128)(2,1)S(1)} %broadcast_select_fusion) | data formatting | bytes 4194304 | tf_op jit(solution)/shard_map/jit(_where)/select_n | solution.py:41
  89.5 5.3 all-to-all-start.1
  94.8 48.2 %all-to-all-done.1 = bf16[2,128,4096]{1,0,2:T(2,128)(2,1)S(1)} async-done(((bf16[2,128,4096]{1,0,2:T(2,128)(2,1)}), bf16[2,128,4096]{1,0,2:T(2,128)(2,1)S(1)}, u32[]{:S(2)}, u32[]{:S(2)}) %all-to-all-start.1) | async-done | bytes 2097184 | tf_op jit(solution)/shard_map/all_to_all | solution.py:42
  144.3 4.7 copy.21
  149.1 2.1 multiply_convert_fusion
  152.6 55.1 %all-gather.5.cloned.1.call-done = bf16[2,4096,512]{2,1,0:T(8,128)(2,1)} async-done(((bf16[2,1024,512]{2,1,0:T(8,128)(2,1)}), bf16[2,4096,512]{2,1,0:T(8,128)(2,1)}) %all-gather.5.cloned.1.call-update) | async-done | bytes 8388624 | tf_op jit(solution)/shard_map/all_gather | solution.py:46
  207.7 230.3 %all-gather.3.cloned.1.call-done = bf16[2,1024,4096]{2,1,0:T(8,128)(2,1)} async-done(((bf16[2,1024,512]{2,1,0:T(8,128)(2,1)}), bf16[2,1024,4096]{2,1,0:T(8,128)(2,1)}) %all-gather.3.cloned.1.call-update) | async-done | bytes 16777232 | tf_op jit(solution)/shard_map/all_gather | solution.py:50
  438.2 58.5 %while.21 = (s32[]{:T(128)}, f32[512,1024]{1,0:T(8,128)S(1)}, s32[]{:T(128)}, s32[2,8]{1,0:T(2,128)S(1)}, bf16[2,1024,4096]{2,1,0:T(8,128)(2,1)}, /*index=5*/bf1...) while((s32[]{:T(128)}, f32[512,1024]{1,0:T(8,128)S(1)}, ...), condition=%wide.region_3.4_spmd, body=%wide.region_2.3_spmd.sunk | while | flops 1085538304 | bytes 11534561 | solution.py:28
  442.7 1.5 dynamic-slice_bitcast_fusion.13
  449.9 1.5 dynamic-slice_bitcast_fusion.13
  457.1 1.5 dynamic-slice_bitcast_fusion.13
  496.8 1.5 neg.13
  498.3 3.0 stack.10
  501.3 1.7 copy.23
  503.3 56.9 %while.20 = (s32[]{:T(128)}, f32[512,1024]{1,0:T(8,128)S(1)}, s32[]{:T(128)}, s32[2,8]{1,0:T(2,128)S(1)}, bf16[2,1024,4096]{2,1,0:T(8,128)(2,1)}, /*index=5*/bf1...) while((s32[]{:T(128)}, f32[512,1024]{1,0:T(8,128)S(1)}, ...), condition=%wide.region_1.2_spmd, body=%wide.region_0.1_spmd.sunk | while | flops 1085538304 | bytes 11534561 | solution.py:28
  560.2 1.5 neg.12
  561.7 3.0 stack.9
  566.3 2.5 pad_maximum_fusion
  (86 shorter events, 75.9 us)
Async XLA Ops:
  6.5 145.4 %copy-start = (s32[2,8,8]{2,1,0:T(8,128)S(1)}, s32[2,8,8]{2,1,0:T(8,128)}, u32[]{:S(2)}) copy-start(s32[2,8,8]{2,1,0:T(8,128)} %param.12) | copy-start | bytes 1540
  11.1 54.0 %all-to-all-start = ((bf16[2,1,128,32,128]{2,4,0,1,3:T(8,128)(2,1)}), bf16[2,1,128,32,128]{2,4,0,1,3:T(8,128)(2,1)}, u32[]{:S(2)}, u32[]{:S(2)}) async-start(bf16[2,1,128,32,128]{2,4,0,1,3:T(8,128)(2,1)} %copy.17), calls=%async_computation | async-start | bytes 4194304 | tf_op jit(solution)/shard_map/all_to_all | solution.py:38
  89.5 53.5 %all-to-all-start.1 = ((bf16[2,128,4096]{1,0,2:T(2,128)(2,1)}), bf16[2,128,4096]{1,0,2:T(2,128)(2,1)S(1)}, u32[]{:S(2)}, u32[]{:S(2)}) async-start(bf16[2,128,4096]{1,0,2:T(2,128)(2,1)} %copy.20), calls=%async_computation.1 | async-start | bytes 4194304 | tf_op jit(solution)/shard_map/all_to_all | solution.py:42
  94.8 112.9 %all-gather.5.cloned.1.call-start = ((), (), s32[]{:S(2)}) async-start(), calls=%async_computation.3 | async-start | bytes 10485760 | tf_op jit(solution)/shard_map/all_gather | solution.py:46
  143.0 1.3 copy-start.3
  144.3 4.7 dynamic-slice-start
  149.1 2.1 copy-start.2
  151.1 0.8 copy-start.5
  151.2 286.8 %all-gather.3.cloned.1.call-start = ((), (), s32[]{:S(2)}) async-start(), calls=%async_computation.2 | async-start | bytes 18874368 | tf_op jit(solution)/shard_map/all_gather | solution.py:50
  564.8 1.6 copy-start.4
  566.3 2.5 copy-start.1
Sparse Core Ops, SparseCore 0:
  151.3 56.3 all-gather.4
  209.7 228.1 all-gather.2
where the time goes:
time: 578 us; the launch traced here: 576 us
  waiting for transfers between devices  379 us (66%)
  local copies, waits for them, and re-layouts  67.9 us (12%)
  loops' own time  42.4 us (7%)
  other arithmetic  39.8 us (7%)
  matrix products  21.2 us (4%)
  between operations  13.6 us (2%)
  starting transfers between devices  11.5 us (2%)
    all_gather x1, waiting for transfers between devices, local(): row_data = lax.all_gather(tile_block, 'rcv', axis=2, tiled=True)  230 us
    all_gather x1, waiting for transfers between devices, local(): column_data = lax.all_gather(weighted, 'src', axis=1, tiled=True)  55.1 us
    all_to_all x1, waiting for transfers between devices, local(): lax.all_to_all(filled, 'rcv', split_axis=2, concat_axis=1, tiled=True)  48.2 us
    all_to_all x1, waiting for transfers between devices, local(): lax.all_to_all(blocks, ('src', 'rcv'), split_axis=3, concat_axis=1, tiled...  45 us
    another operation x2, loops' own time, predict_tile(): return -lax.fori_loop(0, slot_count, add_slot, initial)  42.4 us
    squeeze x16, local copies, waits for them, and re-layouts, complex_product(): left_wide = jnp.concatenate([left_pair[0], left_pair[1]], axis=1)  23.7 us
    dot_general x16, matrix products, complex_product(): return jnp.dot(left_wide, right_wide, preferred_element_type=jnp.float32)  21.2 us
    neg x16, other arithmetic, complex_product(): lower = jnp.concatenate([-right_pair[1], right_pair[0]], axis=1)  18.7 us
  transfers between devices with their start and end apart: 4, of which 4 were waited for; matrix products, arithmetic and copies ran while one was open for 1% of the time, Pallas kernels for 0%

commit v1 on v0

--- a/solution.py
+++ b/solution.py
@@ -43,7 +43,19 @@
     span = tile_block.shape[1]
     gains = lax.dynamic_slice_in_dim(obliquity, lax.axis_index("src") * span, span)
     weighted = (tile_block.astype(jnp.float32) * gains[None, :, None]).astype(jnp.bfloat16)
-    column_data = lax.all_gather(weighted, "src", axis=1, tiled=True)
+
+    def put_scenes_by_axis(z):
+        shares = lax.axis_size("src")
+        found = [(dev_j, (dev_j + 1) % shares) for dev_j in range(shares)]
+        all_values = [None] * shares
+        all_values[shares - 1] = z
+        for w in range(shares - 2, -1, -1):
+            all_values[w] = lax.ppermute(all_values[w + 1], "src", found)
+        part_next = jnp.concatenate(all_values, 1)
+        x_now = (lax.axis_index("src") + 1) * z.shape[1]
+        return jnp.roll(part_next, x_now, 1)
+
+    column_data = put_scenes_by_axis(weighted)
     rcv_index = lax.axis_index("rcv")
     my_lists = lax.dynamic_index_in_dim(aperture, rcv_index, 1, keepdims=False)
     tile_rows = span // TILE_SIZE

time: 578 us -> 513 us (0.89)
  waiting for transfers between devices: 379 us -> 241 us
  blocking collectives: 0 us -> 53 us
  local copies, waits for them, and re-layouts: 67.9 us -> 94.7 us
    all_gather x1, waiting for transfers between devices: 230 us -> 120 us  [local(): row_data = lax.all_gather(tile_block, 'rcv', axis=2, tiled=True)]
    ppermute x0 -> x3, waiting for transfers between devices: none -> 76.1 us  [put_scenes_by_axis(): all_values[w] = lax.ppermute(all_values[w + 1], 'src', found)]
    all_gather x1 -> x0, waiting for transfers between devices: 55.1 us -> none  [local(): column_data = lax.all_gather(weighted, 'src', axis=1, tiled=True)]
    all_to_all x0 -> x1, blocking collectives: none -> 53 us  [local(): lax.all_to_all(filled, 'rcv', split_axis=2, concat_axis=1, tiled=True)]
    all_to_all x1 -> x0, waiting for transfers between devices: 48.2 us -> none  [local(): lax.all_to_all(filled, 'rcv', split_axis=2, concat_axis=1, tiled=True)]
    unnamed x13 -> x22, local copies, waits for them, and re-layouts: 5.65 us -> 24.1 us
    dynamic_slice x0 -> x1, local copies, waits for them, and re-layouts: none -> 7.32 us  [put_scenes_by_axis(): return jnp.roll(part_next, x_now, 1)]
  transfers between devices with their start and end apart: 4 -> 5, of which waited for: 4 -> 5; matrix products, arithmetic and copies ran while one was open for 1% -> 6% of each run, Pallas kernels for 0% -> 0%
where the time goes in v1:
time: 513 us; the launch traced here: 511 us
  waiting for transfers between devices  241 us (47%)
  local copies, waits for them, and re-layouts  94.7 us (18%)
  blocking collectives  53 us (10%)
  loops' own time  43.3 us (8%)
  other arithmetic  38 us (7%)
  matrix products  21.3 us (4%)
  between operations  13.6 us (3%)
  starting transfers between devices  6.17 us (1%)
    all_gather x1, waiting for transfers between devices, local(): row_data = lax.all_gather(tile_block, 'rcv', axis=2, tiled=True)  120 us
    ppermute x3, waiting for transfers between devices, put_scenes_by_axis(): all_values[w] = lax.ppermute(all_values[w + 1], 'src', found)  76.1 us
    all_to_all x1, blocking collectives, local(): lax.all_to_all(filled, 'rcv', split_axis=2, concat_axis=1, tiled=True)  53 us
    all_to_all x1, waiting for transfers between devices, local(): lax.all_to_all(blocks, ('src', 'rcv'), split_axis=3, concat_axis=1, tiled...  44.9 us
    another operation x2, loops' own time, predict_tile(): return -lax.fori_loop(0, slot_count, add_slot, initial)  43.3 us
    unnamed x22, local copies, waits for them, and re-layouts  24.1 us
    squeeze x16, local copies, waits for them, and re-layouts, complex_product(): left_wide = jnp.concatenate([left_pair[0], left_pair[1]], axis=1)  23.6 us
    dot_general x16, matrix products, complex_product(): return jnp.dot(left_wide, right_wide, preferred_element_type=jnp.float32)  21.3 us
  transfers between devices with their start and end apart: 5, of which 5 were waited for; matrix products, arithmetic and copies ran while one was open for 6% of the time, Pallas kernels for 0%

profile of v1, /device:TPU:6, one launch (start us, length us, event | category | flops | bytes accessed | tf_op | source)
XLA Modules:
  0.0 510.9 jit_solution(4813332350383859077)
XLA Ops:
  6.5 3.1 copy.19
  11.1 6.1 %all-to-all-start = ((bf16[2,1,128,32,128]{2,4,0,1,3:T(8,128)(2,1)}), bf16[2,1,128,32,128]{2,4,0,1,3:T(8,128)(2,1)}, u32[]{:S(2)}, u32[]{:S(2)}) async-start(bf16[2,1,128,32,128]{2,4,0,1,3:T(8,128)(2,1)} %copy.17), calls=%async_computation | async-start | bytes 4194304 | tf_op jit(solution)/shard_map/all_to_all | solution.py:38
  17.3 1.9 broadcast_compare_fusion
  20.2 44.9 %all-to-all-done = bf16[2,1,128,32,128]{2,4,0,1,3:T(8,128)(2,1)} async-done(((bf16[2,1,128,32,128]{2,4,0,1,3:T(8,128)(2,1)}), bf16[2,1,128,32,128]{2,4,0,1,3:T(8,128)(2,1)}, u32[]{:S(2)}, u32[]{:S(2)}) %all-to-all-start) | async-done | bytes 2097184 | tf_op jit(solution)/shard_map/all_to_all | solution.py:38
  65.1 4.1 copy.18
  69.2 2.1 broadcast_select_fusion
  71.3 17.8 %copy.20 = bf16[2,128,4096]{1,0,2:T(2,128)(2,1)S(1)} copy(bf16[2,128,4096]{1,2,0:T(8,128)(2,1)S(1)} %broadcast_select_fusion) | data formatting | bytes 4194304 | tf_op jit(solution)/shard_map/jit(_where)/select_n | solution.py:41
  89.2 53.0 %all_to_all.33 = bf16[2,128,4096]{1,0,2:T(2,128)(2,1)S(1)} all-to-all(bf16[2,128,4096]{1,0,2:T(2,128)(2,1)S(1)} %copy.20), channel_id=1, replica_groups=mesh['src'=4,'rcv'=8] {'rcv'}, dimensions={2} | all-to-all | bytes 4194304 | tf_op jit(solution)/shard_map/all_to_all | solution.py:42
  142.2 3.8 copy.21
  149.3 25.5 %collective-permute-done = bf16[2,1024,512]{2,1,0:T(8,128)(2,1)S(1)} collective-permute-done((bf16[2,1024,512]{2,1,0:T(8,128)(2,1)S(1)}, bf16[2,1024,512]{2,1,0:T(8,128)(2,1)S(1)}, u32[]{:S(2)}, u32[]{:S(2)}) %collective-permute-start) | collective-permute-done | bytes 2097184 | tf_op jit(solution)/shard_map/ppermute | solution.py:53
  174.8 25.6 %collective-permute-done.1 = bf16[2,1024,512]{2,1,0:T(8,128)(2,1)} collective-permute-done((bf16[2,1024,512]{2,1,0:T(8,128)(2,1)S(1)}, bf16[2,1024,512]{2,1,0:T(8,128)(2,1)}, u32[]{:S(2)}, u32[]{:S(2)}) %collective-permute-start.1) | collective-permute-done | bytes 2097184 | tf_op jit(solution)/shard_map/ppermute | solution.py:53
  201.0 25.1 %collective-permute-done.2 = bf16[2,1024,512]{2,1,0:T(8,128)(2,1)} collective-permute-done((bf16[2,1024,512]{2,1,0:T(8,128)(2,1)}, bf16[2,1024,512]{2,1,0:T(8,128)(2,1)}, u32[]{:S(2)}, u32[]{:S(2)}) %collective-permute-start.2) | collective-permute-done | bytes 2097184 | tf_op jit(solution)/shard_map/ppermute | solution.py:53
  226.1 3.1 constant_dynamic-update-slice_fusion.7
  229.2 3.0 constant_dynamic-update-slice_fusion.6
  236.1 3.2 constant_dynamic-update-slice_fusion.3
  239.3 3.1 constant_dynamic-update-slice_fusion.2
  245.3 7.3 %constant_dynamic-slice_fusion.2 = bf16[2,4096,512]{2,1,0:T(8,128)(2,1)} fusion(bf16[2,8192,512]{2,1,0:T(8,128)(2,1)} %constant_dynamic-update-slice_fusion, s32[]{:T(128)S(6)} %select_n.42), kind=kLoop, calls=%fused_computation.48 | loop fusion | bytes 16777220 | tf_op jit(solution)/shard_map/jit(_roll_dynamic)/dynamic_slice | solution.py:56
  252.6 119.8 %all-gather.2.cloned.1.call-done = bf16[2,1024,4096]{2,1,0:T(8,128)(2,1)} async-done(((bf16[2,1024,512]{2,1,0:T(8,128)(2,1)}), bf16[2,1024,4096]{2,1,0:T(8,128)(2,1)}) %all-gather.2.cloned.1.call-update) | async-done | bytes 16777232 | tf_op jit(solution)/shard_map/all_gather | solution.py:62
  372.7 57.9 %while.20 = (s32[]{:T(128)}, f32[512,1024]{1,0:T(8,128)S(1)}, s32[]{:T(128)}, s32[2,8]{1,0:T(2,128)S(1)}, bf16[2,1024,4096]{2,1,0:T(8,128)(2,1)}, /*index=5*/bf1...) while((s32[]{:T(128)}, f32[512,1024]{1,0:T(8,128)S(1)}, ...), condition=%wide.region_1.2_spmd, body=%wide.region_0.1_spmd.sunk | while | flops 1085538304 | bytes 11534553 | solution.py:28
  432.1 3.0 stack.9
  435.1 1.7 copy.22
  437.1 58.4 %while.21 = (s32[]{:T(128)}, f32[512,1024]{1,0:T(8,128)S(1)}, s32[]{:T(128)}, s32[2,8]{1,0:T(2,128)S(1)}, bf16[2,1024,4096]{2,1,0:T(8,128)(2,1)}, /*index=5*/bf1...) while((s32[]{:T(128)}, f32[512,1024]{1,0:T(8,128)S(1)}, ...), condition=%wide.region_3.4_spmd, body=%wide.region_2.3_spmd.sunk | while | flops 1085538304 | bytes 11534553 | solution.py:28
  496.9 3.0 stack.10
  501.6 2.5 pad_maximum_fusion
  (98 shorter events, 91.3 us)
Async XLA Ops:
  6.5 193.8 %copy-start = (s32[2,8,8]{2,1,0:T(8,128)S(1)}, s32[2,8,8]{2,1,0:T(8,128)}, u32[]{:S(2)}) copy-start(s32[2,8,8]{2,1,0:T(8,128)} %param.12) | copy-start | bytes 1540
  11.1 54.0 %all-to-all-start = ((bf16[2,1,128,32,128]{2,4,0,1,3:T(8,128)(2,1)}), bf16[2,1,128,32,128]{2,4,0,1,3:T(8,128)(2,1)}, u32[]{:S(2)}, u32[]{:S(2)}) async-start(bf16[2,1,128,32,128]{2,4,0,1,3:T(8,128)(2,1)} %copy.17), calls=%async_computation | async-start | bytes 4194304 | tf_op jit(solution)/shard_map/all_to_all | solution.py:38
  17.3 355.2 %all-gather.2.cloned.1.call-start = ((), (), s32[]{:S(2)}) async-start(), calls=%async_computation.2 | async-start | bytes 18874368 | tf_op jit(solution)/shard_map/all_gather | solution.py:62
  145.9 1.6 copy-start.2
  147.5 52.8 %copy-start.6 = (s32[2,1]{0,1:T(1,128)S(1)}, s32[2,1]{0,1:T(1,128)}, u32[]{:S(2)}) copy-start(s32[2,1]{0,1:T(1,128)} %param.13) | copy-start | bytes 28
  148.0 1.3 copy-start.3
  149.3 25.5 %collective-permute-start = (bf16[2,1024,512]{2,1,0:T(8,128)(2,1)S(1)}, bf16[2,1024,512]{2,1,0:T(8,128)(2,1)S(1)}, u32[]{:S(2)}, u32[]{:S(2)}) collective-permute-start(bf16[2,1024,512]{2,1,0:T(8,128)(2,1)S(1)} %multiply_convert_fusion), channel_id=1, source_target_pairs={{0,8},{8,16},{16,24},{24,0},{1,9},{9,17},{17,25},{25,1},{2,10},{10... | collective-permute-start | bytes 6291464 | tf_op jit(solution)/shard_map/ppermute | solution.py:53
  174.8 25.6 %collective-permute-start.1 = (bf16[2,1024,512]{2,1,0:T(8,128)(2,1)S(1)}, bf16[2,1024,512]{2,1,0:T(8,128)(2,1)}, u32[]{:S(2)}, u32[]{:S(2)}) collective-permute-start(bf16[2,1024,512]{2,1,0:T(8,128)(2,1)S(1)} %collective-permute-done), channel_id=1, source_target_pairs={{0,8},{8,16},{16,24},{24,0},{1,9},{9,17},{17,25},{25,1},{2,10},{10... | collective-permute-start | bytes 6291464 | tf_op jit(solution)/shard_map/ppermute | solution.py:53
  200.3 25.8 %collective-permute-start.2 = (bf16[2,1024,512]{2,1,0:T(8,128)(2,1)}, bf16[2,1024,512]{2,1,0:T(8,128)(2,1)}, u32[]{:S(2)}, u32[]{:S(2)}) collective-permute-start(bf16[2,1024,512]{2,1,0:T(8,128)(2,1)} %collective-permute-done.1), channel_id=1, source_target_pairs={{0,8},{8,16},{16,24},{24,0},{1,9},{9,17},{17,25},{25,1},{2,10},{10... | collective-permute-start | bytes 6291464 | tf_op jit(solution)/shard_map/ppermute | solution.py:53
  232.2 2.4 copy-start.4
  500.0 1.6 copy-start.5
  501.6 2.5 copy-start.1
Sparse Core Ops, SparseCore 0:
  146.1 226.3 all-gather.1
